TPU v7x, 128 devices: a whole 4x4x4 slice. The times are simulated.
128 devices in a mesh: row: 8 (over z, core), col: 16 (over x, y).
Axes of the slice: x: 4, y: 4, z: 4, core: 2. Of those that a mesh axis runs over, the one named last changes fastest.
Arguments:
- tokens: bfloat16 [1024, 12288], P('row', 'col'), may hold values from -6 to 6
- up_weight: bfloat16 [1024, 49152], P('row', 'col'), may hold values from -0.1875 to 0.1875
- down_weight: bfloat16 [1024, 49152], P('row', 'col'), may hold values from -0.09375 to 0.09375
- up_index: int32 [8, 384], P(None, 'col'), may hold values from 0 to 95, as said below
- down_index: int32 [8, 384], P(None, 'col'), may hold values from 0 to 95, as said below
- up_bias: float32 [49152], P('col'), may hold values from -3 to 3
- down_bias: float32 [12288], P('col'), may hold values from -3 to 3
Outputs:
- mixed: bfloat16 [1024, 12288], P('row', 'col')
Inputs may be any that keep to these rules, and one draw needn't show every extreme that they name: For each block column c the 8 entries up_index[:, c] are distinct, and for each slot s the entries over any 96 consecutive block columns are distinct. For each block row r the 8 entries down_index[:, r] are distinct, and for each slot s the entries over any 96 consecutive block rows are distinct.
All inputs are finite; a program needn't handle non-finite values.
Results may differ from a plain program's by a relative error of at most 0.015.
Values may be sent and summed in bfloat16 or wider, within the bound.
A program may use at most 128 MiB of HBM per device.

v0:
```python
import jax
import jax.numpy as jnp
from jax import lax
from jax.sharding import PartitionSpec as P

BLK = 128
KB = 8


def per_device(tokens, up_weight, down_weight, up_index, down_index, up_bias, down_bias):
    gathered = lax.all_gather(tokens, "col", axis=1, tiled=True)
    tok_rows = gathered.shape[0]
    dblocks = gathered.shape[1] // BLK
    features = gathered.reshape(tok_rows, dblocks, BLK)
    col_blocks = up_weight.shape[1] // BLK
    block_ids = jnp.arange(dblocks, dtype=jnp.int32)
    zero_pre = jnp.zeros((tok_rows, col_blocks, BLK), jnp.float32)
    running = zero_pre
    panel_rows = lax.all_gather(up_weight, "row", axis=0, tiled=True)
    block_count = panel_rows.shape[0] // BLK
    panels = panel_rows.reshape(block_count, BLK, col_blocks, BLK)
    for add_slot_index in range(block_count):
        selector = (up_index[add_slot_index][:, None] == block_ids[None, :]).astype(jnp.bfloat16)
        selected = jnp.einsum(
            "cd,tdk->tck", selector, features, preferred_element_type=jnp.float32
        ).astype(jnp.bfloat16)
        running = running + jnp.einsum(
            "tck,kcn->tcn", selected, panels[add_slot_index], preferred_element_type=jnp.float32
        )
    preact = running
    preact = preact + up_bias.reshape(col_blocks, BLK)[None]
    hidden = jax.nn.gelu(preact, approximate=True).astype(jnp.bfloat16)
    down_full = lax.all_gather(down_weight, "row", axis=0, tiled=True)
    down_grid = down_full.reshape(KB, BLK, col_blocks, BLK)
    totals = jnp.zeros((dblocks, tok_rows, BLK), jnp.float32)
    for slot_index in range(KB):
        product = jnp.einsum(
            "trk,nrk->rtn", hidden, down_grid[slot_index], preferred_element_type=jnp.float32
        )
        placer = (block_ids[:, None] == down_index[slot_index][None, :]).astype(jnp.float32)
        totals = totals + jnp.einsum(
            "dr,rtn->dtn",
            placer,
            product,
            precision=lax.Precision.HIGHEST,
            preferred_element_type=jnp.float32,
        )
    reduced = lax.psum_scatter(
        totals.astype(jnp.bfloat16), "col", scatter_dimension=0, tiled=True
    ).astype(jnp.float32)
    result = jnp.transpose(reduced, (1, 0, 2)).reshape(tok_rows, -1) + down_bias[None]
    return result.astype(jnp.bfloat16)


def solution(mesh):
    placed = (
        P("row", "col"),
        P("row", "col"),
        P("row", "col"),
        P(None, "col"),
        P(None, "col"),
        P("col"),
        P("col"),
    )
    return jax.shard_map(
        per_device, mesh=mesh, in_specs=placed, out_specs=P("row", "col"), check_vma=False
    )
```

profile of v0, /device:TPU:0, one launch (start us, length us, event | category | flops | bytes accessed | tf_op | source)
XLA Modules:
  0.0 308.1 jit_solution(4415510976900336198)
XLA Ops:
  6.5 0.0 all-gather.4.cloned.1.call-start
  6.5 0.7 all-gather.4.cloned.1.call-update
  7.3 0.0 all-gather.6.cloned.1.call-start
  7.3 2.3 copy.47
  9.6 0.0 all-gather.6.cloned.1.call-update
  9.6 0.0 all-gather.8.cloned.1.call-start
  9.7 0.0 copy-done.4
  9.7 1.2 copy.64
  10.9 0.0 all-gather.8.cloned.1.call-update
  10.9 0.0 reduce-scatter.2.cloned.1.call-start
  11.0 0.0 copy-done.7
  11.0 0.0 copy-done.8
  11.0 49.1 %all-gather.4.cloned.1.call-done = bf16[128,12288]{1,0:T(8,128)(2,1)} async-done(((bf16[128,768]{1,0:T(8,128)(2,1)}), bf16[128,12288]{1,0:T(8,128)(2,1)}) %all-gather.4.cloned.1.call-update) | async-done | bytes 3145744 | tf_op jit(solution)/shard_map/all_gather | solution.py:11
  60.1 2.6 copy.100
  62.7 1.5 fusion.30
  64.2 1.5 fusion.28
  65.7 1.5 fusion.27
  67.2 0.6 fusion.26
  67.8 0.6 fusion.25
  68.4 0.6 fusion.24
  69.0 0.6 fusion.23
  69.6 1.5 fusion.29
  71.1 34.9 %all-gather.6.cloned.1.call-done = bf16[1024,3072]{0,1:T(8,128)(2,1)} async-done(((bf16[128,3072]{0,1:T(8,128)(2,1)}), bf16[1024,3072]{0,1:T(8,128)(2,1)}) %all-gather.6.cloned.1.call-update) | async-done | bytes 6291472 | tf_op jit(solution)/shard_map/all_gather | solution.py:19
  106.0 3.4 %fusion.96 = (bf16[128,3072]{0,1:T(8,128)(2,1)S(1)}, bf16[128,3072]{0,1:T(8,128)(2,1)S(1)}, bf16[128,3072]{0,1:T(8,128)(2,1)S(1)}, bf16[128,3072]{0,1:T(8,128)(2...) fusion(bf16[1024,3072]{0,1:T(8,128)(2,1)} %all-gather.6.cloned., ...), kind=kLoop, calls=%fused_computation.123 | loop fusion | bytes 12582912 | tf_op jit(solution)/shard_map/slice | solution.py:28
  109.4 0.0 copy-done.2
  109.4 0.0 copy-start.1
  109.4 0.7 fusion.32
  110.1 0.5 copy-done.1
  110.6 0.7 fusion.34
  111.2 0.5 copy-done
  111.7 0.7 fusion.36
  112.3 0.7 fusion.38
  113.0 0.7 fusion.40
  113.7 0.7 fusion.42
  114.3 0.0 copy-start.3
  114.3 0.0 copy-start.5
  114.3 0.7 fusion.44
  115.0 0.5 copy-done.3
  115.5 0.0 copy-done.5
  115.5 1.3 fusion.7
  116.7 37.0 %all-gather.8.cloned.1.call-done = bf16[1024,3072]{0,1:T(8,128)(2,1)} async-done(((bf16[128,3072]{0,1:T(8,128)(2,1)}), bf16[1024,3072]{0,1:T(8,128)(2,1)}) %all-gather.8.cloned.1.call-update) | async-done | bytes 6291472 | tf_op jit(solution)/shard_map/all_gather | solution.py:33
  153.7 3.4 %fusion.95 = (bf16[128,3072]{0,1:T(8,128)(2,1)S(1)}, bf16[128,3072]{0,1:T(8,128)(2,1)S(1)}, bf16[128,3072]{0,1:T(8,128)(2,1)S(1)}, bf16[128,3072]{0,1:T(8,128)(2...) fusion(bf16[1024,3072]{0,1:T(8,128)(2,1)} %all-gather.8.cloned., ...), kind=kLoop, calls=%fused_computation.122 | loop fusion | bytes 12582912 | tf_op jit(solution)/shard_map/slice | solution.py:38
  157.1 0.4 fusion.103
  157.5 1.5 fusion.104
  159.0 0.4 fusion.102
  159.4 0.4 fusion.101
  159.8 0.4 fusion.100
  160.1 0.4 fusion.99
  160.5 0.4 fusion.98
  160.9 0.4 fusion.97
  161.3 5.7 %fusion.21 = f32[96,128,128]{2,0,1:T(8,128)} fusion(f32[24,128,128]{2,1,0:T(8,128)S(1)} %fusion.97, s32[24]{0:T(128)S(1)} %get-tuple-element.27), kind=kOutput, calls=%fused_computation.23 | convolution fusion | flops 452987136 | bytes 7864416 | tf_op jit(solution)/shard_map/dr,rtn->dtn/dot_general | solution.py:41
  167.0 5.5 %fusion.19 = f32[96,128,128]{2,0,1:T(8,128)} fusion(f32[24,128,128]{2,1,0:T(8,128)S(1)} %fusion.98, s32[24]{0:T(128)S(1)} %get-tuple-element.26), kind=kOutput, calls=%fused_computation.21 | convolution fusion | flops 452987136 | bytes 7864416 | tf_op jit(solution)/shard_map/dr,rtn->dtn/dot_general | solution.py:41
  172.5 5.5 %fusion.17 = f32[96,128,128]{2,0,1:T(8,128)} fusion(f32[24,128,128]{2,1,0:T(8,128)S(1)} %fusion.99, s32[24]{0:T(128)S(1)} %get-tuple-element.25), kind=kOutput, calls=%fused_computation.19 | convolution fusion | flops 452987136 | bytes 7864416 | tf_op jit(solution)/shard_map/dr,rtn->dtn/dot_general | solution.py:41
  178.0 5.5 %fusion.15 = f32[96,128,128]{2,0,1:T(8,128)} fusion(f32[24,128,128]{2,1,0:T(8,128)S(1)} %fusion.100, s32[24]{0:T(128)S(1)} %get-tuple-element.24), kind=kOutput, calls=%fused_computation.17 | convolution fusion | flops 452987136 | bytes 7864416 | tf_op jit(solution)/shard_map/dr,rtn->dtn/dot_general | solution.py:41
  183.5 5.4 %fusion.13 = f32[96,128,128]{2,0,1:T(8,128)} fusion(f32[24,128,128]{2,1,0:T(8,128)S(1)} %fusion.101, s32[24]{0:T(128)S(1)} %get-tuple-element.23), kind=kOutput, calls=%fused_computation.15 | convolution fusion | flops 452987136 | bytes 7864416 | tf_op jit(solution)/shard_map/dr,rtn->dtn/dot_general | solution.py:41
  189.0 5.5 %fusion.11 = f32[96,128,128]{2,0,1:T(8,128)} fusion(f32[24,128,128]{2,1,0:T(8,128)S(1)} %fusion.102, s32[24]{0:T(128)S(1)} %get-tuple-element.22), kind=kOutput, calls=%fused_computation.13 | convolution fusion | flops 452987136 | bytes 7864416 | tf_op jit(solution)/shard_map/dr,rtn->dtn/dot_general | solution.py:41
  194.4 5.5 %fusion.9 = f32[96,128,128]{2,0,1:T(8,128)} fusion(f32[24,128,128]{2,1,0:T(8,128)S(1)} %fusion.103, s32[24]{0:T(128)S(1)} %get-tuple-element.28), kind=kOutput, calls=%fused_computation.11 | convolution fusion | flops 452987136 | bytes 7864416 | tf_op jit(solution)/shard_map/dr,rtn->dtn/dot_general | solution.py:41
  199.9 20.0 %add_convert_fusion = bf16[96,128,128]{2,0,1:T(8,128)(2,1)S(1)} fusion(f32[96,128,128]{2,0,1:T(8,128)} %fusion.9, f32[96,128,128]{2,0,1:T(8,128)} %fusion.11, f32[96,128,128]{2,0,1:T(8,128)} %fusion.13, f32[96,128,128]{2,0,1:T(8,128)} %fusion.15, f32[96,128,128]{2,0,1:T(8,128)} %fusion.17, f32[96,128,128]{2,0,1:T(8,128)} %fusion.21, ...), kind=kOutput, calls=%fused_computation | convolution fusion | flops 465570048 | bytes 48758880 | tf_op jit(solution)/shard_map/dr,rtn->dtn/dot_general | solution.py:41
  219.9 2.9 copy.81
  222.8 0.0 reduce-scatter.2.cloned.1.call-update
  222.8 76.7 %reduce-scatter.2.cloned.1.call-done = bf16[6,128,128]{2,1,0:T(8,128)(2,1)} async-done(((bf16[96,128,128]{2,1,0:T(8,128)(2,1)}), bf16[6,128,128]{2,1,0:T(8,128)(2,1)}) %reduce-scatter.2.cloned.1.call-update) | async-done | bytes 196624 | tf_op jit(solution)/shard_map/reduce_scatter | solution.py:48
  299.5 1.1 copy.82
  300.6 0.2 fusion.46
  300.8 0.8 copy.83
  (9 shorter events, 0.0 us)
Async XLA Ops:
  6.5 3.2 %copy-start.4 = (bf16[128,3072]{1,0:T(8,128)(2,1)S(1)}, bf16[128,3072]{1,0:T(8,128)(2,1)}, u32[]{:S(2)}) copy-start(bf16[128,3072]{1,0:T(8,128)(2,1)} %param.9) | copy-start | bytes 2359300
  6.5 53.6 %all-gather.4.cloned.1.call-start = ((), (), s32[]{:S(2)}) async-start(), calls=%async_computation.1 | async-start | bytes 3342336 | tf_op jit(solution)/shard_map/all_gather | solution.py:11
  7.3 98.7 %all-gather.6.cloned.1.call-start = ((), (), s32[]{:S(2)}) async-start(), calls=%async_computation.2 | async-start | bytes 7077888 | tf_op jit(solution)/shard_map/all_gather | solution.py:19
  9.6 1.3 copy-start.7
  9.6 1.4 copy-start.8
  9.6 144.1 %all-gather.8.cloned.1.call-start = ((), (), s32[]{:S(2)}) async-start(), calls=%async_computation.3 | async-start | bytes 7077888 | tf_op jit(solution)/shard_map/all_gather | solution.py:33
  10.9 288.6 %reduce-scatter.2.cloned.1.call-start = ((), (), s32[]{:S(2)}) async-start(), calls=%async_computation.4 | async-start | bytes 3342336 | tf_op jit(solution)/shard_map/reduce_scatter | solution.py:48
  106.0 3.4 %copy-start.2 = (bf16[128,24,128]{2,1,0:T(8,128)(2,1)S(1)}, bf16[128,24,128]{2,1,0:T(8,128)(2,1)}, u32[]{:S(2)}) copy-start(bf16[128,24,128]{2,1,0:T(8,128)(2,1)} %fusion.29) | copy-start | bytes 2359300
  109.4 1.1 copy-start.1
  110.6 1.1 copy-start
  114.3 1.1 copy-start.3
  114.3 1.1 copy-start.5
  222.8 77.8 %copy-start.6 = (f32[768]{0:T(1024)S(1)}, f32[768]{0:T(1024)}, u32[]{:S(2)}) copy-start(f32[768]{0:T(1024)} %param.13) | copy-start | bytes 9220
Sparse Core Ops, SparseCore 0:
  9.6 50.4 all-gather.3
  61.8 44.1 all-gather.5
  107.7 46.0 all-gather.7
  222.9 76.5 reduce-scatter.1
where the time goes:
time: 308 us
  waiting for transfers between devices  198 us (64%)
  matrix products  77 us (25%)
  local copies, waits for them, and re-layouts  19.1 us (6%)
  between operations  13.3 us (4%)
    reduce_scatter x1, waiting for transfers between devices, per_device(): lax.psum_scatter(totals.astype(jnp.bfloat16), 'col', scatter_dimension=0,...  76.7 us
    dot_general x8, matrix products, per_device(): jnp.einsum('dr,rtn->dtn', placer, product, precision=lax.Precision.HIGHES...  58.6 us
    all_gather x1, waiting for transfers between devices, per_device(): gathered = lax.all_gather(tokens, 'col', axis=1, tiled=True)  49.1 us
    all_gather x1, waiting for transfers between devices, per_device(): down_full = lax.all_gather(down_weight, 'row', axis=0, tiled=True)  37 us
    all_gather x1, waiting for transfers between devices, per_device(): panel_rows = lax.all_gather(up_weight, 'row', axis=0, tiled=True)  34.9 us
    dot_general x8, matrix products, per_device(): jnp.einsum('cd,tdk->tck', selector, features, preferred_element_type=jnp....  8.36 us
    unnamed x21, local copies, waits for them, and re-layouts  7.5 us
  transfers between devices with their start and end apart: 4, of which 4 were waited for; matrix products, arithmetic and copies ran while one was open for 8% of the time, Pallas kernels for 0%

commit v1 on v0

v1 whole, which is shorter than its diff:
```python
import jax
import jax.numpy as jnp
from jax import lax
from jax.experimental import pallas as pl
from jax.experimental.pallas import tpu as pltpu
from jax.sharding import PartitionSpec as P

BLK = 128
KB = 8
N = 4
DB = 96
CB = 24
OB = 6
HB = 3
TOK = 128
Q = 4
CH = BLK // Q
HH = CH // 2
NSEM = 220
MESH = pl.DeviceIdType.MESH
F32 = jnp.float32
BF16 = jnp.bfloat16


def kernel(up_idx, inv, tok, up, dn, ub, db, out,
           feat, wu, wd, acc, ht, prod, outp, r1, o2, r2, res, ssem, rsem, lsem):
    row = lax.axis_index("row")
    col = lax.axis_index("col")
    z, k = row // 2, row % 2
    x, y = col // N, col % N
    slot = lambda dz: ((z + dz + N) % N) * 2 + k
    cidx = lambda dx, dy: ((x + dx + N) % N) * N + (y + dy + N) % N
    zp, zm, pr = (slot(1), col), (slot(-1), col), (z * 2 + 1 - k, col)
    xp, xm = (row, cidx(1, 0)), (row, cidx(-1, 0))
    yp, ym = (row, cidx(0, 1)), (row, cidx(0, -1))

    local = []

    def lcopy(src, dst):
        c = pltpu.make_async_copy(src, dst, lsem.at[len(local)])
        c.start()
        local.append(c)
        return c

    tok_in = [lcopy(tok.at[:, pl.ds(j * BLK, BLK)], feat.at[col * OB + j]) for j in range(OB)]
    up_in = lcopy(up, wu.at[row])
    dn_in = lcopy(dn, wd.at[row])

    barrier = pltpu.get_barrier_semaphore()
    for dev in (zp, zm, pr, xp, xm, yp, ym):
        pl.semaphore_signal(barrier, inc=1, device_id=dev, device_id_type=MESH)
    pl.semaphore_wait(barrier, 7)

    sent = []

    def rcopy(src, dst, dev):
        i = len(sent)
        c = pltpu.make_async_remote_copy(
            src_ref=src, dst_ref=dst, send_sem=ssem.at[i], recv_sem=rsem.at[i],
            device_id=dev, device_id_type=MESH)
        c.start()
        sent.append(c)
        return c

    def same(ref, dev):
        return rcopy(ref, ref, dev)

    half = BLK // 2
    ur = lambda h: pl.ds(h * half, half)
    u_p = [rcopy(up.at[ur(h)], wu.at[row, ur(h)], zp) for h in (0, 1)]
    u_m = [rcopy(up.at[ur(h)], wu.at[row, ur(h)], zm) for h in (1, 0)]
    u_c = rcopy(up, wu.at[row], pr)

    for c in tok_in:
        c.wait()

    def chunk(h, da, db_):
        dx, dy = (da, db_) if h == 0 else (db_, da)
        return pl.ds(cidx(dx, dy) * OB + h * HB, HB)

    ax1 = ((xp, xm), (yp, ym))
    ax2 = ((yp, ym), (xp, xm))
    t_own = [[same(feat.at[chunk(h, 0, 0)], d) for d in ax1[h]] for h in (0, 1)]
    t2 = [[[], []], [[], []]]

    def spread(h, da):
        for i, d in enumerate(ax2[h]):
            t2[h][i].append(same(feat.at[chunk(h, da, 0)], d))

    for h in (0, 1):
        spread(h, 0)

    dr = lambda q: pl.ds(q * CH, CH)
    d_own = {}

    def d_issue(q):
        if q < Q:
            d_own[q] = [rcopy(dn.at[dr(q)], wd.at[row, dr(q)], d) for d in (zp, zm)]

    d_issue(0)
    d_c = rcopy(dn, wd.at[row], pr)

    tr = lambda i: pl.ds(i * (TOK // 2), TOK // 2)
    t_fwd = [[], []]
    for h in (0, 1):
        for i in (0, 1):
            t_own[h][i].wait_recv()
            da = -1 if i == 0 else 1
            t_fwd[h].append(same(feat.at[chunk(h, da, 0), tr(i)], ax1[h][i]))
        spread(h, -1)
        spread(h, 1)
    for h in (0, 1):
        for c in t_fwd[h]:
            c.wait_recv()
        spread(h, 2)

    u_p[0].wait_recv()
    u_m[0].wait_recv()
    u_f = [same(wu.at[slot(-1), ur(0)], zp), same(wu.at[slot(1), ur(1)], zm)]
    d_issue(1)

    t2_fwd = [[], []]
    for n, da in enumerate((0, -1, 1, 2)):
        for h in (0, 1):
            for i in (0, 1):
                t2[h][i][n].wait_recv()
                t2_fwd[h].append(
                    same(feat.at[chunk(h, da, -1 if i == 0 else 1), tr(i)], ax2[h][i]))

    prod[:, CB] = jnp.zeros((KB, CH, TOK), F32)
    u_p[1].wait_recv()
    u_m[1].wait_recv()
    u_n = [same(wu.at[slot(-1)], pr), same(wu.at[slot(1)], pr)]
    for h in (0, 1):
        for c in t2_fwd[h]:
            c.wait_recv()
    up_in.wait()
    u_c.wait_recv()
    for c in u_n:
        c.wait_recv()

    zpair = lambda dz: (z + dz + N) % N

    def up_dot(p, c):
        xs = jnp.concatenate([feat[up_idx[2 * p, c]], feat[up_idx[2 * p + 1, c]]], axis=1)
        w = wu[pl.ds(2 * p, 2), :, pl.ds(pl.multiple_of(c * BLK, BLK), BLK)]
        return jnp.dot(xs, w.reshape(2 * BLK, BLK), preferred_element_type=F32)

    def up_first(c, carry):
        acc[c] = up_dot(zpair(0), c) + up_dot(zpair(-1), c) + up_dot(zpair(1), c)
        return carry

    lax.fori_loop(0, CB, up_first, 0)

    d_fwd, d_n, d_far = {}, {}, {}
    hr = lambda q, i: pl.ds(q * CH + i * HH, HH)

    def d_near(q):
        for c in d_own[q]:
            c.wait_recv()
        d_fwd[q] = [same(wd.at[slot(-1), hr(q, 0)], zp), same(wd.at[slot(1), hr(q, 1)], zm)]
        d_issue(q + 2)
        d_n[q] = [same(wd.at[slot(-1), dr(q)], pr), same(wd.at[slot(1), dr(q)], pr)]

    d_near(0)
    for c in u_f:
        c.wait_recv()
    u_far = same(wu.at[slot(2)], pr)
    u_far.wait_recv()

    def up_last(c, carry):
        cols = pl.ds(pl.multiple_of(c * BLK, BLK), BLK)
        v = acc[c] + up_dot(zpair(2), c) + ub[:, cols]
        g = 0.5 * v * (1.0 + jnp.tanh(0.7978845608028654 * (v + 0.044715 * (v * v * v))))
        ht[c] = g.T.astype(BF16)
        return carry

    lax.fori_loop(0, CB, up_last, 0)

    def down_dot(q, p, r):
        w = wd[pl.ds(2 * p, 2), dr(q), pl.ds(pl.multiple_of(r * BLK, BLK), BLK)]
        o = jnp.dot(w.reshape(2 * CH, BLK), ht[r], preferred_element_type=F32)
        prod[pl.ds(2 * p, 2), r] = o.reshape(2, CH, TOK)

    def down_near(q):
        def body(r, carry):
            for dz in (0, -1, 1):
                down_dot(q, zpair(dz), r)
            return carry
        lax.fori_loop(0, CB, body, 0)

    def down_far(q):
        def body(r, carry):
            down_dot(q, zpair(2), r)
            return carry
        lax.fori_loop(0, CB, body, 0)

    def place(q):
        def body(g, carry):
            for j in range(OB):
                d = g * OB + j
                v = prod[0, inv[0, d]]
                for s in range(1, KB):
                    v = v + prod[s, inv[s, d]]
                v = v.astype(BF16)
                for i in (0, 1):
                    outp[q, i, g // N, g % N, j] = v[i * HH:(i + 1) * HH]
            return carry
        lax.fori_loop(0, N * N, body, 0)

    rs1, rs2 = {}, {}
    rx1 = ((yp, ym), (xp, xm))
    rx2 = ((xp, xm), (yp, ym))
    apos = lambda h, da: ((y if h == 0 else x) + da + N) % N
    bpos = lambda h, da: ((x if h == 0 else y) + da + N) % N

    def src1(q, h, da, i):
        if h == 0:
            return outp.at[q, i, :, apos(h, da), pl.ds(0, HB)]
        return outp.at[q, i, apos(h, da), :, pl.ds(HB, HB)]

    def src2(q, h, da, i):
        return o2.at[q, h, i, bpos(h, da)]

    def open_ring(q, h, src, buf, dirs, book):
        p, m = dirs[h]
        book[q, h] = {
            0: rcopy(src(q, h, 2, 0), buf.at[q, h, 0], p),
            1: rcopy(src(q, h, 2, 1), buf.at[q, h, 1], m),
            3: rcopy(src(q, h, 1, 1), buf.at[q, h, 3], p),
            4: rcopy(src(q, h, -1, 0), buf.at[q, h, 4], m),
        }

    def turn_ring(q, h, src, buf, dirs, book):
        p, m = dirs[h]
        b = book[q, h]
        for got, da, i, to, dev in ((0, 1, 0, 2, p), (1, -1, 1, 5, m)):
            b[got].wait_recv()
            s = src(q, h, da, i)
            s[...] = (s[...].astype(F32) + buf[q, h, got].astype(F32)).astype(BF16)
            b[to] = rcopy(s, buf.at[q, h, to], dev)

    def close_ring(q, h, src, buf, book, i):
        a, b = (2, 4) if i == 0 else (3, 5)
        book[q, h][a].wait_recv()
        book[q, h][b].wait_recv()
        return (src(q, h, 0, i)[...].astype(F32) + buf[q, h, a].astype(F32)
                + buf[q, h, b].astype(F32))

    def rs_a(q):
        for h in (0, 1):
            open_ring(q, h, src1, r1, rx1, rs1)

    def rs_b(q):
        for h in (0, 1):
            turn_ring(q, h, src1, r1, rx1, rs1)

    def rs_c(q):
        for h in (0, 1):
            for i in (0, 1):
                o2[q, h, i] = close_ring(q, h, src1, r1, rs1, i).astype(BF16)
            open_ring(q, h, src2, r2, rx2, rs2)

    def rs_d(q):
        for h in (0, 1):
            turn_ring(q, h, src2, r2, rx2, rs2)

    def rs_e(q):
        for h in (0, 1):
            for i in (0, 1):
                res[pl.ds(h * HB, HB), hr(q, i)] = close_ring(q, h, src2, r2, rs2, i)

    dn_in.wait()
    d_c.wait_recv()
    for q in range(Q):
        if q > 0:
            d_near(q)
        for c in d_n[q]:
            c.wait_recv()
        down_near(q)
        if q > 0:
            rs_b(q - 1)
        for c in d_fwd[q]:
            c.wait_recv()
        d_far[q] = same(wd.at[slot(2), dr(q)], pr)
        if q > 0:
            rs_c(q - 1)
        d_far[q].wait_recv()
        down_far(q)
        place(q)
        rs_a(q)
        if q > 0:
            rs_d(q - 1)
            rs_e(q - 1)
    rs_b(Q - 1)
    rs_c(Q - 1)
    rs_d(Q - 1)
    rs_e(Q - 1)

    for j in range(OB):
        cols = pl.ds(j * BLK, BLK)
        out[:, cols] = (res[j].T + db[:, cols]).astype(BF16)
    for c in sent:
        c.wait_send()


def per_device(tokens, up_weight, down_weight, up_index, down_index, up_bias, down_bias):
    rows = jnp.arange(CB, dtype=jnp.int32)
    blocks = jnp.arange(DB, dtype=jnp.int32)
    hit = down_index[:, None, :] == blocks[None, :, None]
    inv = jnp.min(jnp.where(hit, rows[None, None, :], CB), axis=2)
    smem = pl.BlockSpec(memory_space=pltpu.SMEM)
    vmem = pl.BlockSpec(memory_space=pltpu.VMEM)
    hbm = pl.BlockSpec(memory_space=pl.ANY)
    return pl.pallas_call(
        kernel,
        out_shape=jax.ShapeDtypeStruct(tokens.shape, BF16),
        in_specs=[smem, smem, hbm, hbm, hbm, vmem, vmem],
        out_specs=vmem,
        scratch_shapes=[
            pltpu.VMEM((DB, TOK, BLK), BF16),
            pltpu.VMEM((KB, BLK, CB * BLK), BF16),
            pltpu.VMEM((KB, BLK, CB * BLK), BF16),
            pltpu.VMEM((CB, TOK, BLK), F32),
            pltpu.VMEM((CB, BLK, TOK), BF16),
            pltpu.VMEM((KB, CB + 1, CH, TOK), F32),
            pltpu.VMEM((Q, 2, N, N, OB, HH, TOK), BF16),
            pltpu.VMEM((Q, 2, 6, N, HB, HH, TOK), BF16),
            pltpu.VMEM((Q, 2, 2, N, HB, HH, TOK), BF16),
            pltpu.VMEM((Q, 2, 6, HB, HH, TOK), BF16),
            pltpu.VMEM((OB, BLK, TOK), F32),
            pltpu.SemaphoreType.DMA((NSEM,)),
            pltpu.SemaphoreType.DMA((NSEM,)),
            pltpu.SemaphoreType.DMA((8,)),
        ],
        compiler_params=pltpu.CompilerParams(
            collective_id=0, has_side_effects=True, vmem_limit_bytes=60 * 2**20),
    )(up_index, inv, tokens, up_weight, down_weight,
      up_bias.reshape(1, -1), down_bias.reshape(1, -1))


def solution(mesh):
    placed = (
        P("row", "col"),
        P("row", "col"),
        P("row", "col"),
        P(None, "col"),
        P(None, "col"),
        P("col"),
        P("col"),
    )
    return jax.shard_map(
        per_device, mesh=mesh, in_specs=placed, out_specs=P("row", "col"), check_vma=False
    )
```

time: 308 us -> 132 us (0.43)
  waiting for transfers between devices: 198 us -> 0 us
  Pallas kernels: 0 us -> 128 us
  matrix products: 77 us -> 0 us
  local copies, waits for them, and re-layouts: 19.1 us -> 2.9 us
  between operations: 13.3 us -> 0.01 us
    pallas_call x0 -> x1, Pallas kernels: none -> 128 us  [per_device(): pl.pallas_call(kernel, out_shape=jax.ShapeDtypeStruct(tokens.shape, BF16)...]
    all_gather x3 -> x0, waiting for transfers between devices: 121 us -> none  [the longest x1 49.1 us: per_device(): gathered = lax.all_gather(tokens, 'col', axis=1, tiled=True)]
    dot_general x32 -> x0, matrix products: 77 us -> none  [the longest x8 58.6 us: per_device(): jnp.einsum('dr,rtn->dtn', placer, product, precision=lax.Precision.HIGHES...]
    reduce_scatter x1 -> x0, waiting for transfers between devices: 76.7 us -> none  [per_device(): lax.psum_scatter(totals.astype(jnp.bfloat16), 'col', scatter_dimension=0,...]
    slice x2 -> x0, local copies, waits for them, and re-layouts: 6.78 us -> none  [the longest x1 3.43 us: per_device(): panels[add_slot_index]]
    unnamed x21 -> x3, local copies, waits for them, and re-layouts: 7.5 us -> 1.62 us
    convert_element_type x2 -> x0, local copies, waits for them, and re-layouts: 3.69 us -> none  [the longest x1 2.86 us: per_device(): totals.astype(jnp.bfloat16)]
  transfers between devices with their start and end apart: 4 -> 0, of which waited for: 4 -> 0; matrix products, arithmetic and copies ran while one was open for 8% -> 0% of each run, Pallas kernels for 0% -> 0%
where the time goes in v1:
time: 132 us
  Pallas kernels  128 us (97%)
  local copies, waits for them, and re-layouts  2.9 us (2%)
    pallas_call x1, Pallas kernels, per_device(): pl.pallas_call(kernel, out_shape=jax.ShapeDtypeStruct(tokens.shape, BF16)...  128 us

profile of v1, /device:TPU:0, one launch (start us, length us, event | category | flops | bytes accessed | tf_op | source)
XLA Modules:
  0.0 131.8 jit_solution(1904287307664375996)
XLA Ops:
  0.0 0.0 copy-start
  0.0 1.3 reshape.8.db
  1.3 0.0 copy-done
  1.3 0.7 select_reduce_fusion.inv
  2.0 128.1 %shard_map.73 = bf16[128,768]{1,0:T(8,128)(2,1)} custom-call(s32[8,24]{1,0:T(8,128)} %up_idx.1, s32[8,96]{1,0:T(8,128)} %select_reduce_fusion.inv, bf16[128,768]{1,0:T(8,128)(2,1)} %tok.1, bf16[128,3072]{1,0:T(8,128)(2,1)} %up.1, bf16[128,3072]{1,0:T(8,128)(2,1)} %dn.1, f32[1,3072]{1,0:T(1,128)} %bitcast.1, f32[1,768]{1,0:T(1,128)} %reshape.8.db), custom_call_target="tpu_custom_call" | custom-call | tf_op jit(solution)/shard_map/pallas_call | solution.py:315
  130.1 1.6 %copy.9 = bf16[128,768]{1,0:T(8,128)(2,1)} copy(bf16[128,768]{1,0:T(8,128)(2,1)} %shard_map.73) | data formatting | bytes 393216
Async XLA Ops:
  0.0 1.3 copy-start

commit v2 on v1

v2 whole, which is shorter than its diff:
```python
import jax
import jax.numpy as jnp
from jax import lax
from jax.experimental import pallas as pl
from jax.experimental.pallas import tpu as pltpu
from jax.sharding import PartitionSpec as P

BLK = 128
KB = 8
N = 4
DB = 96
CB = 24
OB = 6
HB = 3
TOK = 128
SIZES = (32, 32, 32, 16, 16)
STARTS = tuple(sum(SIZES[:q]) for q in range(len(SIZES)))
Q = len(SIZES)
CH = max(SIZES)
NSEM = 180
UP_UNROLL = 4
DN_UNROLL = 8
MESH = pl.DeviceIdType.MESH
F32 = jnp.float32
BF16 = jnp.bfloat16


def kernel(up_idx, dn_idx, tok, up, dn, ub, out,
           feat, wu, wd, acc, ht, prod, psum, outp, r1, o2, r2, res, inv_v, inv,
           ssem, rsem, lsem):
    row = lax.axis_index("row")
    col = lax.axis_index("col")
    z, k = row // 2, row % 2
    x, y = col // N, col % N
    slot = lambda dz: ((z + dz + N) % N) * 2 + k
    zpair = lambda dz: (z + dz + N) % N
    cidx = lambda dx, dy: ((x + dx + N) % N) * N + (y + dy + N) % N
    zp, zm, pr = (slot(1), col), (slot(-1), col), (z * 2 + 1 - k, col)
    xd = {d: (row, cidx(d, 0)) for d in (1, -1, 2)}
    yd = {d: (row, cidx(0, d)) for d in (1, -1, 2)}
    RING = (1, -1, 2)

    local = []

    def lcopy(src, dst):
        c = pltpu.make_async_copy(src, dst, lsem.at[len(local)])
        c.start()
        local.append(c)
        return c

    tok_in = [lcopy(tok.at[:, pl.ds(j * BLK, BLK)], feat.at[col * OB + j]) for j in range(OB)]
    up_in = lcopy(up, wu.at[row])
    dn_in = lcopy(dn, wd.at[row])

    barrier = pltpu.get_barrier_semaphore()
    peers = [zp, zm, pr] + list(xd.values()) + list(yd.values())
    for dev in peers:
        pl.semaphore_signal(barrier, inc=1, device_id=dev, device_id_type=MESH)

    lanes = lax.broadcasted_iota(jnp.int32, (KB, BLK), 1)
    where = jnp.full((KB, BLK), CB, jnp.int32)
    for r in range(CB):
        where = jnp.where(dn_idx[:, r:r + 1] == lanes, r, where)
    inv_v[...] = where
    prod[:, CB] = jnp.zeros((KB, CH, TOK), F32)

    pl.semaphore_wait(barrier, len(peers))

    sent = []

    def rcopy(src, dst, dev):
        i = len(sent)
        c = pltpu.make_async_remote_copy(
            src_ref=src, dst_ref=dst, send_sem=ssem.at[i], recv_sem=rsem.at[i],
            device_id=dev, device_id_type=MESH)
        c.start()
        sent.append(c)
        return c

    def same(ref, dev):
        return rcopy(ref, ref, dev)

    half = BLK // 2
    ur = lambda h: pl.ds(h * half, half)
    u_p = [rcopy(up.at[ur(h)], wu.at[row, ur(h)], zp) for h in (0, 1)]
    u_m = [rcopy(up.at[ur(h)], wu.at[row, ur(h)], zm) for h in (1, 0)]
    u_c = rcopy(up, wu.at[row], pr)

    for c in tok_in:
        c.wait()

    def chunk(h, da):
        dx, dy = (da, 0) if h == 0 else (0, da)
        return pl.ds(cidx(dx, dy) * OB + h * HB, HB)

    ring1, ring2 = (xd, yd), (yd, xd)
    t1 = [[same(feat.at[chunk(h, 0)], ring1[h][d]) for d in RING] for h in (0, 1)]
    t2 = [[], []]

    def spread(h, da):
        t2[h] += [same(feat.at[chunk(h, da)], ring2[h][d]) for d in RING]

    for h in (0, 1):
        spread(h, 0)
    for n, d in enumerate(RING):
        for h in (0, 1):
            t1[h][n].wait_recv()
            spread(h, -d)

    u_p[0].wait_recv()
    u_m[0].wait_recv()
    u_f = [same(wu.at[slot(-1), ur(0)], zp), same(wu.at[slot(1), ur(1)], zm)]

    dr = lambda q: pl.ds(STARTS[q], SIZES[q])
    d_own, d_fwd, d_n, d_far = {}, {}, {}, {}

    def d_issue(q):
        if q < Q:
            d_own[q] = [rcopy(dn.at[dr(q)], wd.at[row, dr(q)], d) for d in (zp, zm)]

    hc = lambda i: pl.ds(i * (CB * BLK // 2), CB * BLK // 2)

    def d_near(q):
        if q < Q:
            for c in d_own[q]:
                c.wait_recv()
            d_fwd[q] = [same(wd.at[slot(-1), dr(q), hc(0)], zp),
                        same(wd.at[slot(1), dr(q), hc(1)], zm)]
            d_issue(q + 2)
            d_n[q] = [same(wd.at[slot(-1), dr(q)], pr), same(wd.at[slot(1), dr(q)], pr)]

    d_issue(0)
    d_issue(1)
    d_c = rcopy(dn, wd.at[row], pr)

    inv_in = lcopy(inv_v, inv)
    u_p[1].wait_recv()
    u_m[1].wait_recv()
    u_n = [same(wu.at[slot(-1)], pr), same(wu.at[slot(1)], pr)]
    for h in (0, 1):
        for c in t2[h]:
            c.wait_recv()
    up_in.wait()
    u_c.wait_recv()
    for c in u_n:
        c.wait_recv()

    def cols(c):
        return pl.ds(pl.multiple_of(c * BLK, BLK), BLK)

    def up_dot(p, c):
        xs = jnp.concatenate([feat[up_idx[2 * p, c]], feat[up_idx[2 * p + 1, c]]], axis=1)
        w = wu[pl.ds(2 * p, 2), :, cols(c)]
        return jnp.dot(xs, w.reshape(2 * BLK, BLK), preferred_element_type=F32)

    def up_first(c, carry):
        acc[c] = up_dot(zpair(0), c) + up_dot(zpair(-1), c) + up_dot(zpair(1), c)
        return carry

    lax.fori_loop(0, CB, up_first, 0, unroll=UP_UNROLL)

    for c in u_f:
        c.wait_recv()
    u_far = same(wu.at[slot(2)], pr)
    u_far.wait_recv()

    def up_last(c, carry):
        v = acc[c] + up_dot(zpair(2), c) + ub[:, cols(c)]
        g = 0.5 * v * (1.0 + jnp.tanh(0.7978845608028654 * (v + 0.044715 * (v * v * v))))
        ht[c] = g.T.astype(BF16)
        return carry

    lax.fori_loop(0, CB, up_last, 0, unroll=UP_UNROLL)

    def down_dots(q, dzs):
        n = SIZES[q]

        def body(r, carry):
            w = jnp.concatenate(
                [wd[pl.ds(2 * zpair(dz), 2), dr(q), cols(r)].reshape(2 * n, BLK) for dz in dzs],
                axis=0)
            o = jnp.dot(w, ht[r], preferred_element_type=F32)
            for i, dz in enumerate(dzs):
                prod[pl.ds(2 * zpair(dz), 2), r, pl.ds(0, n)] = (
                    o[2 * n * i:2 * n * (i + 1)].reshape(2, n, TOK))
            return carry

        lax.fori_loop(0, CB, body, 0, unroll=DN_UNROLL)

    near, far = (0, -1, 1), (2,)

    def placed(q, d, dzs):
        terms = []
        for dz in dzs:
            for i in (0, 1):
                s = 2 * zpair(dz) + i
                terms.append(prod[s, inv[s, d], pl.ds(0, SIZES[q])])
        while len(terms) > 1:
            terms = [a + b for a, b in zip(terms[::2], terms[1::2])] + (
                [terms[-1]] if len(terms) % 2 else [])
        return terms[0]

    def place_near(q):
        def body(g, carry):
            for j in range(OB):
                d = g * OB + j
                psum[d, pl.ds(0, SIZES[q])] = placed(q, d, near)
            return carry
        lax.fori_loop(0, N * N, body, 0)

    def place_far(q):
        def body(g, carry):
            for j in range(OB):
                d = g * OB + j
                v = psum[d, pl.ds(0, SIZES[q])] + placed(q, d, far)
                outp[g // N, g % N, j, dr(q)] = v.astype(BF16)
            return carry
        lax.fori_loop(0, N * N, body, 0)

    rs1, rs2 = {}, {}

    def src1(q, h, da):
        if h == 0:
            return outp.at[:, (y + da + N) % N, pl.ds(0, HB), dr(q)]
        return outp.at[(x + da + N) % N, :, pl.ds(HB, HB), dr(q)]

    def src2(q, h, db):
        return o2.at[h, ((x if h == 0 else y) + db + N) % N, :, dr(q)]

    def rs_a(q):
        for n, d in enumerate(RING):
            for h in (0, 1):
                rs1[q, h, n] = rcopy(src1(q, h, d), r1.at[h, n, :, :, dr(q)], ring2[h][d])

    def rs_b(q):
        for h in (0, 1):
            total = src1(q, h, 0)[...].astype(F32)
            for n in range(3):
                rs1[q, h, n].wait_recv()
                total = total + r1[h, n, :, :, dr(q)].astype(F32)
            o2[h, :, :, dr(q)] = total.astype(BF16)
            for n, d in enumerate(RING):
                rs2[q, h, n] = rcopy(src2(q, h, d), r2.at[h, n, :, dr(q)], ring1[h][d])

    def rs_c(q):
        for h in (0, 1):
            total = src2(q, h, 0)[...].astype(F32)
            for n in range(3):
                rs2[q, h, n].wait_recv()
                total = total + r2[h, n, :, dr(q)].astype(F32)
            res[pl.ds(h * HB, HB), dr(q)] = total

    inv_in.wait()
    dn_in.wait()
    d_c.wait_recv()
    d_near(0)
    for q in range(Q):
        for c in d_n[q]:
            c.wait_recv()
        down_dots(q, near)
        place_near(q)
        d_near(q + 1)
        if q > 0:
            rs_b(q - 1)
        for c in d_fwd[q]:
            c.wait_recv()
        d_far[q] = same(wd.at[slot(2), dr(q)], pr)
        d_far[q].wait_recv()
        down_dots(q, far)
        place_far(q)
        rs_a(q)
        if q > 0:
            rs_c(q - 1)
    rs_b(Q - 1)
    rs_c(Q - 1)

    for j in range(OB):
        out[:, pl.ds(j * BLK, BLK)] = res[j].T
    for c in sent:
        c.wait_send()


def per_device(tokens, up_weight, down_weight, up_index, down_index, up_bias, down_bias):
    smem = pl.BlockSpec(memory_space=pltpu.SMEM)
    vmem = pl.BlockSpec(memory_space=pltpu.VMEM)
    hbm = pl.BlockSpec(memory_space=pl.ANY)
    total = pl.pallas_call(
        kernel,
        out_shape=jax.ShapeDtypeStruct(tokens.shape, F32),
        in_specs=[smem, vmem, hbm, hbm, hbm, vmem],
        out_specs=vmem,
        scratch_shapes=[
            pltpu.VMEM((DB, TOK, BLK), BF16),
            pltpu.VMEM((KB, BLK, CB * BLK), BF16),
            pltpu.VMEM((KB, BLK, CB * BLK), BF16),
            pltpu.VMEM((CB, TOK, BLK), F32),
            pltpu.VMEM((CB, BLK, TOK), BF16),
            pltpu.VMEM((KB, CB + 1, CH, TOK), F32),
            pltpu.VMEM((DB, CH, TOK), F32),
            pltpu.VMEM((N, N, OB, BLK, TOK), BF16),
            pltpu.VMEM((2, 3, N, HB, BLK, TOK), BF16),
            pltpu.VMEM((2, N, HB, BLK, TOK), BF16),
            pltpu.VMEM((2, 3, HB, BLK, TOK), BF16),
            pltpu.VMEM((OB, BLK, TOK), F32),
            pltpu.VMEM((KB, BLK), jnp.int32),
            pltpu.SMEM((KB, BLK), jnp.int32),
            pltpu.SemaphoreType.DMA((NSEM,)),
            pltpu.SemaphoreType.DMA((NSEM,)),
            pltpu.SemaphoreType.DMA((9,)),
        ],
        compiler_params=pltpu.CompilerParams(
            collective_id=0, has_side_effects=True, vmem_limit_bytes=48 * 2**20),
    )(up_index, down_index, tokens, up_weight, down_weight, up_bias.reshape(1, -1))
    return (total + down_bias[None]).astype(BF16)


def solution(mesh):
    placed = (
        P("row", "col"),
        P("row", "col"),
        P("row", "col"),
        P(None, "col"),
        P(None, "col"),
        P("col"),
        P("col"),
    )
    return jax.shard_map(
        per_device, mesh=mesh, in_specs=placed, out_specs=P("row", "col"), check_vma=False
    )
```

time: 132 us -> 102 us (0.77)
  Pallas kernels: 128 us -> 95.8 us
  local copies, waits for them, and re-layouts: 2.9 us -> 5.27 us
    pallas_call x1, Pallas kernels: 128 us -> 95.8 us  [per_device(): pl.pallas_call(kernel, out_shape=jax.ShapeDtypeStruct(tokens.shape, F32),...]
    unnamed x3 -> x14, local copies, waits for them, and re-layouts: 1.62 us -> 5.27 us
where the time goes in v2:
time: 102 us
  Pallas kernels  95.8 us (94%)
  local copies, waits for them, and re-layouts  5.27 us (5%)
    pallas_call x1, Pallas kernels, per_device(): pl.pallas_call(kernel, out_shape=jax.ShapeDtypeStruct(tokens.shape, F32),...  95.8 us
    unnamed x14, local copies, waits for them, and re-layouts  5.27 us

profile of v2, /device:TPU:0, one launch (start us, length us, event | category | flops | bytes accessed | tf_op | source)
XLA Modules:
  0.0 101.8 jit_solution(11229680909815794513)
XLA Ops:
  0.0 0.0 copy-start
  0.0 1.1 %copy-done = bf16[128,3072]{1,0:T(8,128)(2,1)S(1)} copy-done((bf16[128,3072]{1,0:T(8,128)(2,1)S(1)}, bf16[128,3072]{1,0:T(8,128)(2,1)}, u32[]{:S(2)}) %copy-start) | copy-done | bytes 786456
  1.1 0.0 copy-start.1
  1.1 1.1 %copy-done.1 = bf16[128,3072]{1,0:T(8,128)(2,1)S(1)} copy-done((bf16[128,3072]{1,0:T(8,128)(2,1)S(1)}, bf16[128,3072]{1,0:T(8,128)(2,1)}, u32[]{:S(2)}) %copy-start.1) | copy-done | bytes 786456
  2.3 0.0 copy-start.2
  2.3 0.9 copy-done.2
  3.2 0.0 copy-start.3
  3.2 0.7 copy-done.3
  3.9 0.0 copy-start.4
  3.9 0.7 copy-done.4
  4.6 0.0 copy-start.5
  4.6 0.7 copy-done.5
  5.3 0.0 copy-start.6
  5.3 95.8 %shard_map.73 = f32[128,768]{1,0:T(8,128)S(1)} custom-call(s32[8,24]{1,0:T(8,128)S(1)} %copy-done.4, s32[8,24]{1,0:T(8,128)S(1)} %copy-done.5, bf16[128,768]{1,0:T(8,128)(2,1)S(1)} %copy-done.2, bf16[128,3072]{1,0:T(8,128)(2,1)S(1)} %copy-done, bf16[128,3072]{1,0:T(8,128)(2,1)S(1)} %copy-done.1, f32[1,3072]{1,0:T(1,128)S(1)} %bitcast.1), custom_call_target="tpu_custom_call" | custom-call | tf_op jit(solution)/shard_map/pallas_call | solution.py:287
  101.1 0.0 copy-done.6
  101.1 0.7 add_convert_fusion
Async XLA Ops:
  0.0 1.1 %copy-start = (bf16[128,3072]{1,0:T(8,128)(2,1)S(1)}, bf16[128,3072]{1,0:T(8,128)(2,1)}, u32[]{:S(2)}) copy-start(bf16[128,3072]{1,0:T(8,128)(2,1)} %up.1) | copy-start | bytes 2359300
  1.1 1.1 %copy-start.1 = (bf16[128,3072]{1,0:T(8,128)(2,1)S(1)}, bf16[128,3072]{1,0:T(8,128)(2,1)}, u32[]{:S(2)}) copy-start(bf16[128,3072]{1,0:T(8,128)(2,1)} %dn.1) | copy-start | bytes 2359300
  2.3 0.9 copy-start.2
  3.2 0.7 copy-start.3
  3.9 0.7 copy-start.4
  4.6 0.7 copy-start.5
  5.3 95.8 %copy-start.6 = (f32[768]{0:T(1024)S(1)}, f32[768]{0:T(1024)}, u32[]{:S(2)}) copy-start(f32[768]{0:T(1024)} %param.13) | copy-start | bytes 9220

commit v3 on v2

--- a/solution.py
+++ b/solution.py
@@ -170,7 +170,9 @@
         ht[c] = g.T.astype(BF16)
         return carry
 
-    lax.fori_loop(0, CB, up_last, 0, unroll=UP_UNROLL)
+    lax.fori_loop(0, CB // 2, up_last, 0, unroll=UP_UNROLL)
+    d_near(0)
+    lax.fori_loop(CB // 2, CB, up_last, 0, unroll=UP_UNROLL)
 
     def down_dots(q, dzs):
         n = SIZES[q]
@@ -253,18 +255,19 @@
     inv_in.wait()
     dn_in.wait()
     d_c.wait_recv()
-    d_near(0)
     for q in range(Q):
         for c in d_n[q]:
             c.wait_recv()
         down_dots(q, near)
-        place_near(q)
-        d_near(q + 1)
-        if q > 0:
-            rs_b(q - 1)
+        if q == 0:
+            d_near(1)
         for c in d_fwd[q]:
             c.wait_recv()
         d_far[q] = same(wd.at[slot(2), dr(q)], pr)
+        d_near(q + 2)
+        place_near(q)
+        if q > 0:
+            rs_b(q - 1)
         d_far[q].wait_recv()
         down_dots(q, far)
         place_far(q)

time: 102 us -> 99.7 us (0.977)
  Pallas kernels: 95.8 us -> 93.3 us
    pallas_call x1, Pallas kernels: 95.8 us -> 93.3 us  [per_device(): pl.pallas_call(kernel, out_shape=jax.ShapeDtypeStruct(tokens.shape, F32),...]
where the time goes in v3:
time: 99.7 us; the launch traced here: 99.3 us
  Pallas kernels  93.3 us (94%)
  local copies, waits for them, and re-layouts  5.27 us (5%)
    pallas_call x1, Pallas kernels, per_device(): pl.pallas_call(kernel, out_shape=jax.ShapeDtypeStruct(tokens.shape, F32),...  93.3 us
    unnamed x14, local copies, waits for them, and re-layouts  5.27 us

profile of v3, /device:TPU:0, one launch (start us, length us, event | category | flops | bytes accessed | tf_op | source)
XLA Modules:
  0.0 99.3 jit_solution(9090308893510961247)
XLA Ops:
  0.0 0.0 copy-start
  0.0 1.1 %copy-done = bf16[128,3072]{1,0:T(8,128)(2,1)S(1)} copy-done((bf16[128,3072]{1,0:T(8,128)(2,1)S(1)}, bf16[128,3072]{1,0:T(8,128)(2,1)}, u32[]{:S(2)}) %copy-start) | copy-done | bytes 786456
  1.1 0.0 copy-start.1
  1.1 1.1 %copy-done.1 = bf16[128,3072]{1,0:T(8,128)(2,1)S(1)} copy-done((bf16[128,3072]{1,0:T(8,128)(2,1)S(1)}, bf16[128,3072]{1,0:T(8,128)(2,1)}, u32[]{:S(2)}) %copy-start.1) | copy-done | bytes 786456
  2.3 0.0 copy-start.2
  2.3 0.9 copy-done.2
  3.2 0.0 copy-start.3
  3.2 0.7 copy-done.3
  3.9 0.0 copy-start.4
  3.9 0.7 copy-done.4
  4.6 0.0 copy-start.5
  4.6 0.7 copy-done.5
  5.3 0.0 copy-start.6
  5.3 93.3 %shard_map.73 = f32[128,768]{1,0:T(8,128)S(1)} custom-call(s32[8,24]{1,0:T(8,128)S(1)} %copy-done.4, s32[8,24]{1,0:T(8,128)S(1)} %copy-done.5, bf16[128,768]{1,0:T(8,128)(2,1)S(1)} %copy-done.2, bf16[128,3072]{1,0:T(8,128)(2,1)S(1)} %copy-done, bf16[128,3072]{1,0:T(8,128)(2,1)S(1)} %copy-done.1, f32[1,3072]{1,0:T(1,128)S(1)} %bitcast.1), custom_call_target="tpu_custom_call" | custom-call | tf_op jit(solution)/shard_map/pallas_call | solution.py:290
  98.6 0.0 copy-done.6
  98.6 0.7 add_convert_fusion
Async XLA Ops:
  0.0 1.1 %copy-start = (bf16[128,3072]{1,0:T(8,128)(2,1)S(1)}, bf16[128,3072]{1,0:T(8,128)(2,1)}, u32[]{:S(2)}) copy-start(bf16[128,3072]{1,0:T(8,128)(2,1)} %up.1) | copy-start | bytes 2359300
  1.1 1.1 %copy-start.1 = (bf16[128,3072]{1,0:T(8,128)(2,1)S(1)}, bf16[128,3072]{1,0:T(8,128)(2,1)}, u32[]{:S(2)}) copy-start(bf16[128,3072]{1,0:T(8,128)(2,1)} %dn.1) | copy-start | bytes 2359300
  2.3 0.9 copy-start.2
  3.2 0.7 copy-start.3
  3.9 0.7 copy-start.4
  4.6 0.7 copy-start.5
  5.3 93.3 %copy-start.6 = (f32[768]{0:T(1024)S(1)}, f32[768]{0:T(1024)}, u32[]{:S(2)}) copy-start(f32[768]{0:T(1024)} %param.13) | copy-start | bytes 9220

commit v4 on v3

--- a/solution.py
+++ b/solution.py
@@ -219,6 +219,19 @@
             return carry
         lax.fori_loop(0, N * N, body, 0)
 
+    def place_all(q):
+        def body(g, carry):
+            for j in range(OB):
+                outp[g // N, g % N, j, dr(q)] = placed(q, g * OB + j, near + far).astype(BF16)
+            return carry
+        lax.fori_loop(0, N * N, body, 0)
+
+    def far_send(q):
+        if q < Q:
+            for c in d_fwd[q]:
+                c.wait_recv()
+            d_far[q] = same(wd.at[slot(2), dr(q)], pr)
+
     rs1, rs2 = {}, {}
 
     def src1(q, h, da):
@@ -258,19 +271,23 @@
     for q in range(Q):
         for c in d_n[q]:
             c.wait_recv()
-        down_dots(q, near)
         if q == 0:
+            down_dots(q, near)
             d_near(1)
-        for c in d_fwd[q]:
-            c.wait_recv()
-        d_far[q] = same(wd.at[slot(2), dr(q)], pr)
-        d_near(q + 2)
-        place_near(q)
-        if q > 0:
+            far_send(0)
+            d_near(2)
+            place_near(q)
+            d_far[q].wait_recv()
+            down_dots(q, far)
+            far_send(1)
+            place_far(q)
+        else:
+            d_far[q].wait_recv()
+            down_dots(q, near + far)
+            far_send(q + 1)
+            d_near(q + 2)
             rs_b(q - 1)
-        d_far[q].wait_recv()
-        down_dots(q, far)
-        place_far(q)
+            place_all(q)
         rs_a(q)
         if q > 0:
             rs_c(q - 1)

time: 99.7 us -> 102 us (1.023)
  Pallas kernels: 93.3 us -> 95.9 us
    pallas_call x1, Pallas kernels: 93.3 us -> 95.9 us  [per_device(): pl.pallas_call(kernel, out_shape=jax.ShapeDtypeStruct(tokens.shape, F32),...]
where the time goes in v4:
time: 102 us
  Pallas kernels  95.9 us (94%)
  local copies, waits for them, and re-layouts  5.27 us (5%)
    pallas_call x1, Pallas kernels, per_device(): pl.pallas_call(kernel, out_shape=jax.ShapeDtypeStruct(tokens.shape, F32),...  95.9 us
    unnamed x14, local copies, waits for them, and re-layouts  5.27 us

profile of v4, /device:TPU:0, one launch (start us, length us, event | category | flops | bytes accessed | tf_op | source)
XLA Modules:
  0.0 101.9 jit_solution(3830639865891725572)
XLA Ops:
  0.0 0.0 copy-start
  0.0 1.1 %copy-done = bf16[128,3072]{1,0:T(8,128)(2,1)S(1)} copy-done((bf16[128,3072]{1,0:T(8,128)(2,1)S(1)}, bf16[128,3072]{1,0:T(8,128)(2,1)}, u32[]{:S(2)}) %copy-start) | copy-done | bytes 786456
  1.1 0.0 copy-start.1
  1.1 1.1 %copy-done.1 = bf16[128,3072]{1,0:T(8,128)(2,1)S(1)} copy-done((bf16[128,3072]{1,0:T(8,128)(2,1)S(1)}, bf16[128,3072]{1,0:T(8,128)(2,1)}, u32[]{:S(2)}) %copy-start.1) | copy-done | bytes 786456
  2.3 0.0 copy-start.2
  2.3 0.9 copy-done.2
  3.2 0.0 copy-start.3
  3.2 0.7 copy-done.3
  3.9 0.0 copy-start.4
  3.9 0.7 copy-done.4
  4.6 0.0 copy-start.5
  4.6 0.7 copy-done.5
  5.3 0.0 copy-start.6
  5.3 95.9 %shard_map.73 = f32[128,768]{1,0:T(8,128)S(1)} custom-call(s32[8,24]{1,0:T(8,128)S(1)} %copy-done.4, s32[8,24]{1,0:T(8,128)S(1)} %copy-done.5, bf16[128,768]{1,0:T(8,128)(2,1)S(1)} %copy-done.2, bf16[128,3072]{1,0:T(8,128)(2,1)S(1)} %copy-done, bf16[128,3072]{1,0:T(8,128)(2,1)S(1)} %copy-done.1, f32[1,3072]{1,0:T(1,128)S(1)} %bitcast.1), custom_call_target="tpu_custom_call" | custom-call | tf_op jit(solution)/shard_map/pallas_call | solution.py:307
  101.2 0.0 copy-done.6
  101.2 0.7 add_convert_fusion
Async XLA Ops:
  0.0 1.1 %copy-start = (bf16[128,3072]{1,0:T(8,128)(2,1)S(1)}, bf16[128,3072]{1,0:T(8,128)(2,1)}, u32[]{:S(2)}) copy-start(bf16[128,3072]{1,0:T(8,128)(2,1)} %up.1) | copy-start | bytes 2359300
  1.1 1.1 %copy-start.1 = (bf16[128,3072]{1,0:T(8,128)(2,1)S(1)}, bf16[128,3072]{1,0:T(8,128)(2,1)}, u32[]{:S(2)}) copy-start(bf16[128,3072]{1,0:T(8,128)(2,1)} %dn.1) | copy-start | bytes 2359300
  2.3 0.9 copy-start.2
  3.2 0.7 copy-start.3
  3.9 0.7 copy-start.4
  4.6 0.7 copy-start.5
  5.3 95.9 %copy-start.6 = (f32[768]{0:T(1024)S(1)}, f32[768]{0:T(1024)}, u32[]{:S(2)}) copy-start(f32[768]{0:T(1024)} %param.13) | copy-start | bytes 9220
